TPU v7x, 256 devices: a whole 4x4x8 slice. The times are simulated.
256 devices in a mesh: row: 32 (over z, x_lo, core), col: 8 (over y, x_hi).
Axes of the slice: x: 4 (x_hi: 2, x_lo: 2; x = x_hi * 2 + x_lo), y: 4, z: 8, core: 2. Of those that a mesh axis runs over, the one named last changes fastest.
Arguments:
- x0_rows: bfloat16 [8192, 32768], P('row', 'col'), may hold values from -0.125 to 0.125
- x1_rows: bfloat16 [8192, 32768], P('row', 'col'), may hold values from -0.125 to 0.125
- x0_cols: bfloat16 [32768, 6144], P('row', 'col'), may hold values from -6 to 6
- x1_cols: bfloat16 [32768, 6144], P('row', 'col'), may hold values from -6 to 6
- mask0_rows: int32 [64, 256], P('row', 'col'), may hold values 0 or 1
- mask1_rows: int32 [64, 256], P('row', 'col'), may hold values 0 or 1
- mask0_cols: int32 [256, 48], P('row', 'col'), may hold values 0 or 1
- mask1_cols: int32 [256, 48], P('row', 'col'), may hold values 0 or 1
- keep_mask: int32 [64, 48], P('row', 'col'), may hold values 0 or 1
Outputs:
- x_square: bfloat16 [8192, 6144], P('row', 'col')
- x_tangent: bfloat16 [8192, 6144], P('row', 'col')
All inputs are finite; a program needn't handle non-finite values. No bound on the sum of `mask0_rows` or of `mask1_rows` or of `mask0_cols` or of `mask1_cols` or of `keep_mask` on one device may be relied on, other than what follows from the above.
Results may differ from a plain program's by a relative error of at most 0.001.
Values may be sent and summed in bfloat16 or wider, within the bound.
A program may use at most 128 MiB of HBM per device.

v0:
```python
import jax
import jax.numpy as jnp
from jax import lax
from jax.sharding import PartitionSpec as P

BLOCK = 128


def passed_along(shard, axis, by):
    devices = lax.axis_size(axis)
    return lax.ppermute(shard, axis, [(i, (i + by) % devices) for i in range(devices)])


def masked(values, mask):
    rows_b, cols_b = mask.shape
    tiles = values.reshape(rows_b, BLOCK, cols_b, BLOCK)
    return (tiles * mask.astype(values.dtype)[:, None, :, None]).reshape(values.shape)


def per_device(
    x0_rows, x1_rows, x0_cols, x1_cols, mask0_rows, mask1_rows, mask0_cols, mask1_cols, keep_mask
):
    n_row = lax.axis_size("row")
    n_col = lax.axis_size("col")
    group = n_row // n_col
    row_index = lax.axis_index("row")
    col_index = lax.axis_index("col")
    panel = x0_cols.shape[0]
    start = row_index % group * panel
    block_start = row_index % group * (panel // BLOCK)
    left_zero = masked(
        lax.dynamic_slice_in_dim(x0_rows, start, panel, 1),
        lax.dynamic_slice_in_dim(mask0_rows, block_start, panel // BLOCK, 1),
    )
    left_one = masked(
        lax.dynamic_slice_in_dim(x1_rows, start, panel, 1),
        lax.dynamic_slice_in_dim(mask1_rows, block_start, panel // BLOCK, 1),
    )
    right_zero = masked(x0_cols, mask0_cols)
    right_one = masked(x1_cols, mask1_cols)
    left = jnp.stack([left_zero, left_one])
    right = jnp.stack([right_zero, right_one])
    left_offset = row_index // group % n_col
    right_offset = col_index % n_col
    levels = n_col.bit_length() - 1
    for level in range(levels):
        moved_left = passed_along(left, "col", -(1 << level))
        moved_right = passed_along(right, "row", -group * (1 << level))
        left = jnp.where(left_offset // (1 << level) % 2 == 1, moved_left, left)
        right = jnp.where(right_offset // (1 << level) % 2 == 1, moved_right, right)

    def accumulate(left_now, right_now, square, tangent):
        square = square + jnp.dot(left_now[0], right_now[0], preferred_element_type=jnp.float32)
        tangent = tangent + jnp.dot(left_now[0], right_now[1], preferred_element_type=jnp.float32)
        tangent = tangent + jnp.dot(left_now[1], right_now[0], preferred_element_type=jnp.float32)
        return (square, tangent)

    def section_body(section, carry):
        left_now, right_now, square, tangent = carry
        square, tangent = accumulate(left_now, right_now, square, tangent)
        left_now = passed_along(left_now, "col", -1)
        right_now = passed_along(right_now, "row", -group)
        return (left_now, right_now, square, tangent)

    zeros = jnp.zeros((left_zero.shape[0], right_zero.shape[1]), jnp.float32)
    left, right, square, tangent = lax.fori_loop(
        0, n_col - 1, section_body, (left, right, zeros, zeros)
    )
    square, tangent = accumulate(left, right, square, tangent)
    x_square = masked(square, keep_mask).astype(jnp.bfloat16)
    x_tangent = masked(tangent, keep_mask).astype(jnp.bfloat16)
    return (x_square, x_tangent)


def solution(mesh):
    return jax.shard_map(
        per_device,
        mesh=mesh,
        in_specs=(
            P("row", "col"),
            P("row", "col"),
            P("row", "col"),
            P("row", "col"),
            P("row", "col"),
            P("row", "col"),
            P("row", "col"),
            P("row", "col"),
            P("row", "col"),
        ),
        out_specs=(P("row", "col"), P("row", "col")),
        check_vma=False,
    )
```

profile of v0, /device:TPU:6, one launch (start us, length us, event | category | flops | bytes accessed | tf_op | source)
XLA Modules:
  0.0 876.7 jit_solution(9657054423650000025)
XLA Ops:
  10.8 5.9 collective-permute-start.5
  16.7 67.7 %collective-permute-done.5 = bf16[2,1024,768]{1,2,0:T(8,128)(2,1)} collective-permute-done((bf16[2,1024,768]{1,2,0:T(8,128)(2,1)}, bf16[2,1024,768]{1,2,0:T(8,128)(2,1)}, u32[]{:S(2)}, u32[]{:S(2)}) %collective-permute-start.5) | collective-permute-done | bytes 3145760 | tf_op jit(solution)/shard_map/ppermute | solution.py:11
  95.2 95.6 %collective-permute-done.6 = bf16[2,1024,768]{1,2,0:T(8,128)(2,1)} collective-permute-done((bf16[2,1024,768]{1,2,0:T(8,128)(2,1)}, bf16[2,1024,768]{1,2,0:T(8,128)(2,1)}, u32[]{:S(2)}, u32[]{:S(2)}) %collective-permute-start.6) | collective-permute-done | bytes 3145760 | tf_op jit(solution)/shard_map/ppermute | solution.py:11
  194.1 4.4 collective-permute-start.7
  199.9 4.0 collective-permute-start.3
  203.9 21.7 %collective-permute-done.3 = bf16[2,256,1024]{2,1,0:T(8,128)(2,1)S(1)} collective-permute-done((bf16[2,256,1024]{2,1,0:T(8,128)(2,1)S(1)}, bf16[2,256,1024]{2,1,0:T(8,128)(2,1)S(1)}, u32[]{:S(2)}, u32[]{:S(2)}) %collective-permute-start.3) | collective-permute-done | bytes 1048608 | tf_op jit(solution)/shard_map/ppermute | solution.py:11
  229.9 20.9 %collective-permute-done.4 = bf16[2,256,1024]{2,1,0:T(8,128)(2,1)S(1)} collective-permute-done((bf16[2,256,1024]{2,1,0:T(8,128)(2,1)S(1)}, bf16[2,256,1024]{2,1,0:T(8,128)(2,1)S(1)}, u32[]{:S(2)}, u32[]{:S(2)}) %collective-permute-start.4) | collective-permute-done | bytes 1048608 | tf_op jit(solution)/shard_map/ppermute | solution.py:11
  251.9 83.6 %collective-permute-done.7 = bf16[2,1024,768]{1,2,0:T(8,128)(2,1)} collective-permute-done((bf16[2,1024,768]{1,2,0:T(8,128)(2,1)}, bf16[2,1024,768]{1,2,0:T(8,128)(2,1)}, u32[]{:S(2)}, u32[]{:S(2)}) %collective-permute-start.7) | collective-permute-done | bytes 3145760 | tf_op jit(solution)/shard_map/ppermute | solution.py:11
  340.6 527.8 %while.17 = (s32[]{:T(128)}, bf16[2,256,1024]{2,1,0:T(8,128)(2,1)}, bf16[2,1024,768]{2,1,0:T(8,128)(2,1)}, f32[256,768]{1,0:T(8,128)}, f32[256,768]{1,0:T(8,128)}, /*index=5*/s32[]{:T(128)}, s32[]{:T(128)}) while((s32[]{:T(128)}, bf16[2,256,1024]{2,1,0:T(8,128)(2,1)}, bf16[2,1024,768]{2,1,0:T(8,128)(2,1)}, f32[256,768]{1,0:T(8,128)}, ...), condition=%wide.region_1.2_spmd.clone, body=%wide.region_0.1_spmd.clone.sunk | while | flops 1208942592 | bytes 42467548 | solution.py:66
  342.5 38.8 %collective-permute-start.1 = (bf16[2,1024,768]{2,1,0:T(8,128)(2,1)S(1)}, bf16[2,1024,768]{2,1,0:T(8,128)(2,1)}, u32[]{:S(2)}, u32[]{:S(2)}) collective-permute-start(bf16[2,1024,768]{2,1,0:T(8,128)(2,1)S(1)} %copy.37), channel_id=1, source_target_pairs={{0,224},{8,232},{16,240},{24,248},{32,0},{40,8},{48,16},{56,24},{6... | collective-permute-start | bytes 9437192 | tf_op jit(solution)/shard_map/while/body/eval_jaxpr/ppermute | solution.py:11
  389.6 21.4 %collective-permute-done = bf16[2,256,1024]{2,1,0:T(8,128)(2,1)} collective-permute-done((bf16[2,256,1024]{2,1,0:T(8,128)(2,1)}, bf16[2,256,1024]{2,1,0:T(8,128)(2,1)}, u32[]{:S(2)}, u32[]{:S(2)}) %collective-permute-start) | collective-permute-done | bytes 1048608 | tf_op jit(solution)/shard_map/while/body/eval_jaxpr/ppermute | solution.py:11
  411.0 37.8 %collective-permute-done.1 = bf16[2,1024,768]{2,1,0:T(8,128)(2,1)} collective-permute-done((bf16[2,1024,768]{2,1,0:T(8,128)(2,1)S(1)}, bf16[2,1024,768]{2,1,0:T(8,128)(2,1)}, u32[]{:S(2)}, u32[]{:S(2)}) %collective-permute-start.1) | collective-permute-done | bytes 3145760 | tf_op jit(solution)/shard_map/while/body/eval_jaxpr/ppermute | solution.py:11
  463.0 20.3 %collective-permute-done = bf16[2,256,1024]{2,1,0:T(8,128)(2,1)} collective-permute-done((bf16[2,256,1024]{2,1,0:T(8,128)(2,1)}, bf16[2,256,1024]{2,1,0:T(8,128)(2,1)}, u32[]{:S(2)}, u32[]{:S(2)}) %collective-permute-start) | collective-permute-done | bytes 1048608 | tf_op jit(solution)/shard_map/while/body/eval_jaxpr/ppermute | solution.py:11
  483.2 37.8 %collective-permute-done.1 = bf16[2,1024,768]{2,1,0:T(8,128)(2,1)} collective-permute-done((bf16[2,1024,768]{2,1,0:T(8,128)(2,1)S(1)}, bf16[2,1024,768]{2,1,0:T(8,128)(2,1)}, u32[]{:S(2)}, u32[]{:S(2)}) %collective-permute-start.1) | collective-permute-done | bytes 3145760 | tf_op jit(solution)/shard_map/while/body/eval_jaxpr/ppermute | solution.py:11
  535.2 19.3 %collective-permute-done = bf16[2,256,1024]{2,1,0:T(8,128)(2,1)} collective-permute-done((bf16[2,256,1024]{2,1,0:T(8,128)(2,1)}, bf16[2,256,1024]{2,1,0:T(8,128)(2,1)}, u32[]{:S(2)}, u32[]{:S(2)}) %collective-permute-start) | collective-permute-done | bytes 1048608 | tf_op jit(solution)/shard_map/while/body/eval_jaxpr/ppermute | solution.py:11
  554.5 37.8 %collective-permute-done.1 = bf16[2,1024,768]{2,1,0:T(8,128)(2,1)} collective-permute-done((bf16[2,1024,768]{2,1,0:T(8,128)(2,1)S(1)}, bf16[2,1024,768]{2,1,0:T(8,128)(2,1)}, u32[]{:S(2)}, u32[]{:S(2)}) %collective-permute-start.1) | collective-permute-done | bytes 3145760 | tf_op jit(solution)/shard_map/while/body/eval_jaxpr/ppermute | solution.py:11
  606.5 18.4 %collective-permute-done = bf16[2,256,1024]{2,1,0:T(8,128)(2,1)} collective-permute-done((bf16[2,256,1024]{2,1,0:T(8,128)(2,1)}, bf16[2,256,1024]{2,1,0:T(8,128)(2,1)}, u32[]{:S(2)}, u32[]{:S(2)}) %collective-permute-start) | collective-permute-done | bytes 1048608 | tf_op jit(solution)/shard_map/while/body/eval_jaxpr/ppermute | solution.py:11
  625.0 37.8 %collective-permute-done.1 = bf16[2,1024,768]{2,1,0:T(8,128)(2,1)} collective-permute-done((bf16[2,1024,768]{2,1,0:T(8,128)(2,1)S(1)}, bf16[2,1024,768]{2,1,0:T(8,128)(2,1)}, u32[]{:S(2)}, u32[]{:S(2)}) %collective-permute-start.1) | collective-permute-done | bytes 3145760 | tf_op jit(solution)/shard_map/while/body/eval_jaxpr/ppermute | solution.py:11
  677.0 17.5 %collective-permute-done = bf16[2,256,1024]{2,1,0:T(8,128)(2,1)} collective-permute-done((bf16[2,256,1024]{2,1,0:T(8,128)(2,1)}, bf16[2,256,1024]{2,1,0:T(8,128)(2,1)}, u32[]{:S(2)}, u32[]{:S(2)}) %collective-permute-start) | collective-permute-done | bytes 1048608 | tf_op jit(solution)/shard_map/while/body/eval_jaxpr/ppermute | solution.py:11
  694.5 37.8 %collective-permute-done.1 = bf16[2,1024,768]{2,1,0:T(8,128)(2,1)} collective-permute-done((bf16[2,1024,768]{2,1,0:T(8,128)(2,1)S(1)}, bf16[2,1024,768]{2,1,0:T(8,128)(2,1)}, u32[]{:S(2)}, u32[]{:S(2)}) %collective-permute-start.1) | collective-permute-done | bytes 3145760 | tf_op jit(solution)/shard_map/while/body/eval_jaxpr/ppermute | solution.py:11
  746.4 16.6 %collective-permute-done = bf16[2,256,1024]{2,1,0:T(8,128)(2,1)} collective-permute-done((bf16[2,256,1024]{2,1,0:T(8,128)(2,1)}, bf16[2,256,1024]{2,1,0:T(8,128)(2,1)}, u32[]{:S(2)}, u32[]{:S(2)}) %collective-permute-start) | collective-permute-done | bytes 1048608 | tf_op jit(solution)/shard_map/while/body/eval_jaxpr/ppermute | solution.py:11
  763.0 37.8 %collective-permute-done.1 = bf16[2,1024,768]{2,1,0:T(8,128)(2,1)} collective-permute-done((bf16[2,1024,768]{2,1,0:T(8,128)(2,1)S(1)}, bf16[2,1024,768]{2,1,0:T(8,128)(2,1)}, u32[]{:S(2)}, u32[]{:S(2)}) %collective-permute-start.1) | collective-permute-done | bytes 3145760 | tf_op jit(solution)/shard_map/while/body/eval_jaxpr/ppermute | solution.py:11
  815.0 15.6 %collective-permute-done = bf16[2,256,1024]{2,1,0:T(8,128)(2,1)} collective-permute-done((bf16[2,256,1024]{2,1,0:T(8,128)(2,1)}, bf16[2,256,1024]{2,1,0:T(8,128)(2,1)}, u32[]{:S(2)}, u32[]{:S(2)}) %collective-permute-start) | collective-permute-done | bytes 1048608 | tf_op jit(solution)/shard_map/while/body/eval_jaxpr/ppermute | solution.py:11
  830.7 37.8 %collective-permute-done.1 = bf16[2,1024,768]{2,1,0:T(8,128)(2,1)} collective-permute-done((bf16[2,1024,768]{2,1,0:T(8,128)(2,1)S(1)}, bf16[2,1024,768]{2,1,0:T(8,128)(2,1)}, u32[]{:S(2)}, u32[]{:S(2)}) %collective-permute-start.1) | collective-permute-done | bytes 3145760 | tf_op jit(solution)/shard_map/while/body/eval_jaxpr/ppermute | solution.py:11
  (140 shorter events, 139.6 us)
Async XLA Ops:
  10.8 73.5 %collective-permute-start.5 = (bf16[2,1024,768]{1,2,0:T(8,128)(2,1)}, bf16[2,1024,768]{1,2,0:T(8,128)(2,1)}, u32[]{:S(2)}, u32[]{:S(2)}) collective-permute-start(bf16[2,1024,768]{1,2,0:T(8,128)(2,1)} %pad_maximum_fusion), channel_id=1, source_target_pairs={{0,224},{8,232},{16,240},{24,248},{32,0},{40,8},{48,16},{56,24},{6... | collective-permute-start | bytes 9437192 | tf_op jit(solution)/shard_map/ppermute | solution.py:11
  16.7 74.5 %copy-start.12 = (s32[2,32]{1,0:T(2,128)S(1)}, s32[2,32]{1,0:T(2,128)}, u32[]{:S(2)}) copy-start(s32[2,32]{1,0:T(2,128)} %param.16) | copy-start | bytes 772
  16.7 74.5 %copy-start.13 = (s32[2,32]{1,0:T(2,128)S(1)}, s32[2,32]{1,0:T(2,128)}, u32[]{:S(2)}) copy-start(s32[2,32]{1,0:T(2,128)} %param.15) | copy-start | bytes 772
  88.3 102.6 %collective-permute-start.6 = (bf16[2,1024,768]{1,2,0:T(8,128)(2,1)}, bf16[2,1024,768]{1,2,0:T(8,128)(2,1)}, u32[]{:S(2)}, u32[]{:S(2)}) collective-permute-start(bf16[2,1024,768]{1,2,0:T(8,128)(2,1)} %broadcast_select_fusion), channel_id=1, source_target_pairs={{0,192},{8,200},{16,208},{24,216},{32,224},{40,232},{48,240},{56,2... | collective-permute-start | bytes 9437192 | tf_op jit(solution)/shard_map/ppermute | solution.py:11
  95.2 103.3 %collective-permute-start.2 = (bf16[2,256,1024]{2,1,0:T(8,128)(2,1)}, bf16[2,256,1024]{2,1,0:T(8,128)(2,1)}, u32[]{:S(2)}, u32[]{:S(2)}) collective-permute-start(bf16[2,256,1024]{2,1,0:T(8,128)(2,1)} %pad_maximum_fusion.1), channel_id=1, source_target_pairs={{0,7},{1,0},{2,1},{3,2},{4,3},{5,4},{6,5},{7,6},{8,15},{9,8},{10,9... | collective-permute-start | bytes 3145736 | tf_op jit(solution)/shard_map/ppermute | solution.py:11
  194.1 141.4 %collective-permute-start.7 = (bf16[2,1024,768]{1,2,0:T(8,128)(2,1)}, bf16[2,1024,768]{1,2,0:T(8,128)(2,1)}, u32[]{:S(2)}, u32[]{:S(2)}) collective-permute-start(bf16[2,1024,768]{1,2,0:T(8,128)(2,1)} %broadcast_select_fusion.1), channel_id=1, source_target_pairs={{0,128},{8,136},{16,144},{24,152},{32,160},{40,168},{48,176},{56,1... | collective-permute-start | bytes 9437192 | tf_op jit(solution)/shard_map/ppermute | solution.py:11
  199.9 25.7 %collective-permute-start.3 = (bf16[2,256,1024]{2,1,0:T(8,128)(2,1)S(1)}, bf16[2,256,1024]{2,1,0:T(8,128)(2,1)S(1)}, u32[]{:S(2)}, u32[]{:S(2)}) collective-permute-start(bf16[2,256,1024]{2,1,0:T(8,128)(2,1)S(1)} %broadcast_select_fusion.3), channel_id=1, source_target_pairs={{0,6},{1,7},{2,0},{3,1},{4,2},{5,3},{6,4},{7,5},{8,14},{9,15},{10,... | collective-permute-start | bytes 3145736 | tf_op jit(solution)/shard_map/ppermute | solution.py:11
  225.8 25.0 %collective-permute-start.4 = (bf16[2,256,1024]{2,1,0:T(8,128)(2,1)S(1)}, bf16[2,256,1024]{2,1,0:T(8,128)(2,1)S(1)}, u32[]{:S(2)}, u32[]{:S(2)}) collective-permute-start(bf16[2,256,1024]{2,1,0:T(8,128)(2,1)S(1)} %broadcast_select_fusion.4), channel_id=1, source_target_pairs={{0,4},{1,5},{2,6},{3,7},{4,0},{5,1},{6,2},{7,3},{8,12},{9,13},{10,... | collective-permute-start | bytes 3145736 | tf_op jit(solution)/shard_map/ppermute | solution.py:11
  342.5 106.2 %collective-permute-start.1 = (bf16[2,1024,768]{2,1,0:T(8,128)(2,1)S(1)}, bf16[2,1024,768]{2,1,0:T(8,128)(2,1)}, u32[]{:S(2)}, u32[]{:S(2)}) collective-permute-start(bf16[2,1024,768]{2,1,0:T(8,128)(2,1)S(1)} %copy.37), channel_id=1, source_target_pairs={{0,224},{8,232},{16,240},{24,248},{32,0},{40,8},{48,16},{56,24},{6... | collective-permute-start | bytes 9437192 | tf_op jit(solution)/shard_map/while/body/eval_jaxpr/ppermute | solution.py:11
  383.6 27.4 %collective-permute-start = (bf16[2,256,1024]{2,1,0:T(8,128)(2,1)}, bf16[2,256,1024]{2,1,0:T(8,128)(2,1)}, u32[]{:S(2)}, u32[]{:S(2)}) collective-permute-start(bf16[2,256,1024]{2,1,0:T(8,128)(2,1)} %copy.36), channel_id=1, source_target_pairs={{0,7},{1,0},{2,1},{3,2},{4,3},{5,4},{6,5},{7,6},{8,15},{9,8},{10,9... | collective-permute-start | bytes 3145736 | tf_op jit(solution)/shard_map/while/body/eval_jaxpr/ppermute | solution.py:11
  389.6 59.1 %copy-start.10 = (f32[256,768]{1,0:T(8,128)}, f32[256,768]{1,0:T(8,128)S(1)}, u32[]{:S(2)}) copy-start(f32[256,768]{1,0:T(8,128)S(1)} %fusion.62) | copy-start | bytes 2359300 | tf_op jit(solution)/shard_map/while
  450.6 70.4 %collective-permute-start.1 = (bf16[2,1024,768]{2,1,0:T(8,128)(2,1)S(1)}, bf16[2,1024,768]{2,1,0:T(8,128)(2,1)}, u32[]{:S(2)}, u32[]{:S(2)}) collective-permute-start(bf16[2,1024,768]{2,1,0:T(8,128)(2,1)S(1)} %copy.37), channel_id=1, source_target_pairs={{0,224},{8,232},{16,240},{24,248},{32,0},{40,8},{48,16},{56,24},{6... | collective-permute-start | bytes 9437192 | tf_op jit(solution)/shard_map/while/body/eval_jaxpr/ppermute | solution.py:11
  456.7 26.5 %collective-permute-start = (bf16[2,256,1024]{2,1,0:T(8,128)(2,1)}, bf16[2,256,1024]{2,1,0:T(8,128)(2,1)}, u32[]{:S(2)}, u32[]{:S(2)}) collective-permute-start(bf16[2,256,1024]{2,1,0:T(8,128)(2,1)} %copy.36), channel_id=1, source_target_pairs={{0,7},{1,0},{2,1},{3,2},{4,3},{5,4},{6,5},{7,6},{8,15},{9,8},{10,9... | collective-permute-start | bytes 3145736 | tf_op jit(solution)/shard_map/while/body/eval_jaxpr/ppermute | solution.py:11
  462.9 58.0 %copy-start.10 = (f32[256,768]{1,0:T(8,128)}, f32[256,768]{1,0:T(8,128)S(1)}, u32[]{:S(2)}) copy-start(f32[256,768]{1,0:T(8,128)S(1)} %fusion.62) | copy-start | bytes 2359300 | tf_op jit(solution)/shard_map/while
  522.9 69.4 %collective-permute-start.1 = (bf16[2,1024,768]{2,1,0:T(8,128)(2,1)S(1)}, bf16[2,1024,768]{2,1,0:T(8,128)(2,1)}, u32[]{:S(2)}, u32[]{:S(2)}) collective-permute-start(bf16[2,1024,768]{2,1,0:T(8,128)(2,1)S(1)} %copy.37), channel_id=1, source_target_pairs={{0,224},{8,232},{16,240},{24,248},{32,0},{40,8},{48,16},{56,24},{6... | collective-permute-start | bytes 9437192 | tf_op jit(solution)/shard_map/while/body/eval_jaxpr/ppermute | solution.py:11
  528.9 25.6 %collective-permute-start = (bf16[2,256,1024]{2,1,0:T(8,128)(2,1)}, bf16[2,256,1024]{2,1,0:T(8,128)(2,1)}, u32[]{:S(2)}, u32[]{:S(2)}) collective-permute-start(bf16[2,256,1024]{2,1,0:T(8,128)(2,1)} %copy.36), channel_id=1, source_target_pairs={{0,7},{1,0},{2,1},{3,2},{4,3},{5,4},{6,5},{7,6},{8,15},{9,8},{10,9... | collective-permute-start | bytes 3145736 | tf_op jit(solution)/shard_map/while/body/eval_jaxpr/ppermute | solution.py:11
  594.2 68.5 %collective-permute-start.1 = (bf16[2,1024,768]{2,1,0:T(8,128)(2,1)S(1)}, bf16[2,1024,768]{2,1,0:T(8,128)(2,1)}, u32[]{:S(2)}, u32[]{:S(2)}) collective-permute-start(bf16[2,1024,768]{2,1,0:T(8,128)(2,1)S(1)} %copy.37), channel_id=1, source_target_pairs={{0,224},{8,232},{16,240},{24,248},{32,0},{40,8},{48,16},{56,24},{6... | collective-permute-start | bytes 9437192 | tf_op jit(solution)/shard_map/while/body/eval_jaxpr/ppermute | solution.py:11
  600.3 24.7 %collective-permute-start = (bf16[2,256,1024]{2,1,0:T(8,128)(2,1)}, bf16[2,256,1024]{2,1,0:T(8,128)(2,1)}, u32[]{:S(2)}, u32[]{:S(2)}) collective-permute-start(bf16[2,256,1024]{2,1,0:T(8,128)(2,1)} %copy.36), channel_id=1, source_target_pairs={{0,7},{1,0},{2,1},{3,2},{4,3},{5,4},{6,5},{7,6},{8,15},{9,8},{10,9... | collective-permute-start | bytes 3145736 | tf_op jit(solution)/shard_map/while/body/eval_jaxpr/ppermute | solution.py:11
  664.6 67.6 %collective-permute-start.1 = (bf16[2,1024,768]{2,1,0:T(8,128)(2,1)S(1)}, bf16[2,1024,768]{2,1,0:T(8,128)(2,1)}, u32[]{:S(2)}, u32[]{:S(2)}) collective-permute-start(bf16[2,1024,768]{2,1,0:T(8,128)(2,1)S(1)} %copy.37), channel_id=1, source_target_pairs={{0,224},{8,232},{16,240},{24,248},{32,0},{40,8},{48,16},{56,24},{6... | collective-permute-start | bytes 9437192 | tf_op jit(solution)/shard_map/while/body/eval_jaxpr/ppermute | solution.py:11
  670.7 23.8 %collective-permute-start = (bf16[2,256,1024]{2,1,0:T(8,128)(2,1)}, bf16[2,256,1024]{2,1,0:T(8,128)(2,1)}, u32[]{:S(2)}, u32[]{:S(2)}) collective-permute-start(bf16[2,256,1024]{2,1,0:T(8,128)(2,1)} %copy.36), channel_id=1, source_target_pairs={{0,7},{1,0},{2,1},{3,2},{4,3},{5,4},{6,5},{7,6},{8,15},{9,8},{10,9... | collective-permute-start | bytes 3145736 | tf_op jit(solution)/shard_map/while/body/eval_jaxpr/ppermute | solution.py:11
  734.1 66.7 %collective-permute-start.1 = (bf16[2,1024,768]{2,1,0:T(8,128)(2,1)S(1)}, bf16[2,1024,768]{2,1,0:T(8,128)(2,1)}, u32[]{:S(2)}, u32[]{:S(2)}) collective-permute-start(bf16[2,1024,768]{2,1,0:T(8,128)(2,1)S(1)} %copy.37), channel_id=1, source_target_pairs={{0,224},{8,232},{16,240},{24,248},{32,0},{40,8},{48,16},{56,24},{6... | collective-permute-start | bytes 9437192 | tf_op jit(solution)/shard_map/while/body/eval_jaxpr/ppermute | solution.py:11
  740.2 22.9 %collective-permute-start = (bf16[2,256,1024]{2,1,0:T(8,128)(2,1)}, bf16[2,256,1024]{2,1,0:T(8,128)(2,1)}, u32[]{:S(2)}, u32[]{:S(2)}) collective-permute-start(bf16[2,256,1024]{2,1,0:T(8,128)(2,1)} %copy.36), channel_id=1, source_target_pairs={{0,7},{1,0},{2,1},{3,2},{4,3},{5,4},{6,5},{7,6},{8,15},{9,8},{10,9... | collective-permute-start | bytes 3145736 | tf_op jit(solution)/shard_map/while/body/eval_jaxpr/ppermute | solution.py:11
  802.7 65.8 %collective-permute-start.1 = (bf16[2,1024,768]{2,1,0:T(8,128)(2,1)S(1)}, bf16[2,1024,768]{2,1,0:T(8,128)(2,1)}, u32[]{:S(2)}, u32[]{:S(2)}) collective-permute-start(bf16[2,1024,768]{2,1,0:T(8,128)(2,1)S(1)} %copy.37), channel_id=1, source_target_pairs={{0,224},{8,232},{16,240},{24,248},{32,0},{40,8},{48,16},{56,24},{6... | collective-permute-start | bytes 9437192 | tf_op jit(solution)/shard_map/while/body/eval_jaxpr/ppermute | solution.py:11
  808.7 21.9 %collective-permute-start = (bf16[2,256,1024]{2,1,0:T(8,128)(2,1)}, bf16[2,256,1024]{2,1,0:T(8,128)(2,1)}, u32[]{:S(2)}, u32[]{:S(2)}) collective-permute-start(bf16[2,256,1024]{2,1,0:T(8,128)(2,1)} %copy.36), channel_id=1, source_target_pairs={{0,7},{1,0},{2,1},{3,2},{4,3},{5,4},{6,5},{7,6},{8,15},{9,8},{10,9... | collective-permute-start | bytes 3145736 | tf_op jit(solution)/shard_map/while/body/eval_jaxpr/ppermute | solution.py:11
  (23 other events, 422.1 us)
where the time goes:
time: 879 us; the launch traced here: 877 us
  waiting for transfers between devices  683 us (78%)
  starting transfers between devices  81.3 us (9%)
  matrix products  50.9 us (6%)
  local copies, waits for them, and re-layouts  40.1 us (5%)
  other arithmetic  20.4 us (2%)
    ppermute x20, waiting for transfers between devices, passed_along(): lax.ppermute(shard, axis, [(i, (i + by) % devices) for i in range(devices)])  683 us
    ppermute x20, starting transfers between devices, passed_along(): lax.ppermute(shard, axis, [(i, (i + by) % devices) for i in range(devices)])  81.3 us
    while x42, local copies, waits for them, and re-layouts  29.1 us
    dot_general x8, matrix products, accumulate(): jnp.dot(left_now[1], right_now[0], preferred_element_type=jnp.float32)  20.5 us
  transfers between devices with their start and end apart: 20, of which 19 were waited for; matrix products, arithmetic and copies ran while one was open for 8% of the time, Pallas kernels for 0%

commit v1 on v0

v1 whole, which is shorter than its diff:
```python
import functools

import jax
import jax.numpy as jnp
from jax import lax
from jax.experimental import pallas as pl
from jax.experimental.pallas import tpu as pltpu
from jax.sharding import PartitionSpec as P

BLOCK = 128
LEVELS = 32760.0
FLOOR = 1e-33
MESH = pl.DeviceIdType.MESH


def kernel(
    group, nz, nc,
    x0_rows, x1_rows, x0_cols, x1_cols, m0_rows, m1_rows, m0_cols, m1_cols, keep,
    out_square, out_tangent,
    own, left, right, part, q_out, q_in, s_out, s_in, stage,
    load_sem, load_right_sem, v_send, left_recv, g_send, q_send, q_recv, s_send, s_recv, store_sem,
):
    rows, depth = own.shape[0] * own.shape[2], own.shape[3]
    piece = own.shape[2]
    cols = right.shape[2]
    half = part.shape[2]
    row = lax.axis_index("row")
    col = lax.axis_index("col")
    z, s = row // group, row % group
    y, xh = col // 2, col % 2
    ny = nc // 2
    partner = y * 2 + 1 - xh
    up_y, down_y = (y + 1) % ny, (y + ny - 1) % ny
    up, down = up_y * 2 + xh, down_y * 2 + xh
    on_diagonal = z == col

    def left_load(which, source, q):
        return pltpu.make_async_copy(
            source.at[pl.ds(q * piece, piece), pl.ds(pl.multiple_of(s * depth, depth), depth)],
            own.at[q, which],
            load_sem.at[which, q],
        )

    def right_load(which, source):
        return pltpu.make_async_copy(source, right.at[which], load_right_sem.at[which])

    for q in range(nc):
        left_load(0, x0_rows, q).start()
        left_load(1, x1_rows, q).start()
    right_load(0, x0_cols).start()
    right_load(1, x1_cols).start()

    barrier = pltpu.get_barrier_semaphore()
    for p in range(nz):

        @pl.when(jnp.logical_or(z != p, z != col))
        def _():
            pl.semaphore_signal(barrier, inc=1, device_id=(p * group + s, z), device_id_type=MESH)

    for c in (partner, up, down):
        pl.semaphore_signal(barrier, inc=1, device_id=(row, c), device_id_type=MESH)
    for zn in ((z + 1) % nz, (z + nz - 1) % nz):
        pl.semaphore_signal(barrier, inc=1, device_id=(zn * group + s, col), device_id_type=MESH)

    for q in range(nc):
        left_load(0, x0_rows, q).wait()
        left_load(1, x1_rows, q).wait()
        for which, mask in enumerate((m0_rows, m1_rows)):
            for j in range(depth // BLOCK):
                keep_it = mask[q * piece // BLOCK, s * (depth // BLOCK) + j].astype(jnp.float32)
                lanes = slice(j * BLOCK, (j + 1) * BLOCK)
                own[q, which, :, lanes] = (own[q, which, :, lanes].astype(jnp.float32) * keep_it).astype(jnp.bfloat16)

    pl.semaphore_wait(barrier, nz + 5 - jnp.where(on_diagonal, 1, 0))

    def scatter(q):
        return pltpu.make_async_remote_copy(
            src_ref=own.at[q],
            dst_ref=left.at[z, q],
            send_sem=v_send.at[q],
            recv_sem=left_recv.at[z, q],
            device_id=(col * group + s, q),
            device_id_type=MESH,
        )

    for q in range(nc):

        @pl.when(jnp.logical_or(z != col, col != q))
        def _():
            scatter(q).start()

    @pl.when(on_diagonal)
    def _():
        left[z, col] = own[col]

    right_load(0, x0_cols).wait()
    right_load(1, x1_cols).wait()

    @pl.loop(0, depth // BLOCK)
    def _(i):
        span = pl.ds(pl.multiple_of(i * BLOCK, BLOCK), BLOCK)
        for which, mask in enumerate((m0_cols, m1_cols)):
            for j in range(cols // BLOCK):
                keep_it = mask[i, j].astype(jnp.float32)
                lanes = slice(j * BLOCK, (j + 1) * BLOCK)
                right[which, span, lanes] = (right[which, span, lanes].astype(jnp.float32) * keep_it).astype(jnp.bfloat16)

    def distance(t):
        return nz // 2 - (t + 1) // 2

    def panel(t):
        ahead = t % 2
        return (z + ahead * distance(t) + (1 - ahead) * (nz - distance(t))) % nz

    def hand_on(t, q, c, k):
        p = panel(t)
        return pltpu.make_async_remote_copy(
            src_ref=left.at[p, q],
            dst_ref=left.at[p, q],
            send_sem=g_send.at[t, k],
            recv_sem=left_recv.at[p, q],
            device_id=(row, c),
            device_id_type=MESH,
        )

    def first(t):
        @pl.when(jnp.logical_or(panel(t) != z, z != col))
        def _():
            hand_on(t, col, partner, 0).wait_recv()

        hand_on(t, col, up, 1).start()
        hand_on(t, col, down, 2).start()
        hand_on(t, col, partner, 0).start()

    def second(t):
        hand_on(t, partner, partner, 0).wait_recv()
        hand_on(t, partner, up, 3).start()
        hand_on(t, partner, down, 4).start()

    from_down, from_up = down_y * 2, up_y * 2 + 1

    def third(t):
        hand_on(t, from_down, up, 5).wait_recv()
        hand_on(t, from_down, up, 5).start()
        hand_on(t, from_up, down, 6).wait_recv()
        hand_on(t, from_up, down, 6).start()

    far_y = (y + 2) % ny

    def rest(t):
        for q in (down_y * 2 + 1, up_y * 2, far_y * 2, far_y * 2 + 1):
            hand_on(t, q, up, 5).wait_recv()

    width = 256 if cols % 256 == 0 else BLOCK

    def products(t):
        p = panel(t)

        @pl.loop(0, cols // width)
        def _(n):
            start = pl.multiple_of(n * width, width)
            l0 = left[p, :, 0].reshape(rows, depth)
            l1 = left[p, :, 1].reshape(rows, depth)
            r0 = right[0, :, pl.ds(start, width)]
            r1 = right[1, :, pl.ds(start, width)]
            square = jnp.dot(l0, r0, preferred_element_type=jnp.float32)
            tangent = jnp.dot(l0, r1, preferred_element_type=jnp.float32)
            tangent = tangent + jnp.dot(l1, r0, preferred_element_type=jnp.float32)
            for h in range(2):
                part[t, h, :, pl.ds(start, width)] = square[h * half : (h + 1) * half]
                part[t, h, :, pl.ds(cols + start, width)] = tangent[h * half : (h + 1) * half]

    def slot_of(way, h, d):
        return (way * 2 + h) * (nz // 2) + d - 1

    def values_copy(way, h, d):
        slot = slot_of(way, h, d)
        zn = (z + 1 + way * (nz - 2)) % nz
        return pltpu.make_async_remote_copy(
            src_ref=q_out.at[slot],
            dst_ref=q_in.at[slot],
            send_sem=q_send.at[slot],
            recv_sem=q_recv.at[slot],
            device_id=(zn * group + s, col),
            device_id_type=MESH,
        )

    def scales_copy(way, h, d):
        slot = slot_of(way, h, d)
        zn = (z + 1 + way * (nz - 2)) % nz
        return pltpu.make_async_remote_copy(
            src_ref=s_out.at[slot],
            dst_ref=s_in.at[slot],
            send_sem=s_send.at[slot],
            recv_sem=s_recv.at[slot],
            device_id=(zn * group + s, col),
            device_id_type=MESH,
        )

    def arrived(way, h, d):
        values_copy(way, h, d).wait_recv()
        scales_copy(way, h, d).wait_recv()

    def decoded(slot, lanes):
        return q_in[slot, :, lanes].astype(jnp.int32).astype(jnp.float32) * s_in[slot, :, lanes]

    def send_on(t, way, h, d, adding):
        slot = slot_of(way, h, d)
        if adding:
            arrived(way, h, d + 1)

        @pl.loop(0, 2 * cols // BLOCK)
        def _(j):
            lanes = pl.ds(pl.multiple_of(j * BLOCK, BLOCK), BLOCK)
            total = part[t, h, :, lanes]
            if adding:
                total = total + decoded(slot + 1, lanes)
            top = jnp.maximum(jnp.max(jnp.abs(total), axis=0, keepdims=True), FLOOR)
            q_out[slot, :, lanes] = jnp.round(total * (LEVELS / top)).astype(jnp.int32).astype(jnp.int16)
            s_out[slot, :, lanes] = top * (1.0 / LEVELS)

        values_copy(way, h, d).start()
        scales_copy(way, h, d).start()

    first(0)
    first(1)
    first(2)
    second(0)
    second(1)
    third(0)

    @pl.loop(0, nz)
    def _(t):
        @pl.when(t + 3 < nz)
        def _():
            first(t + 3)

        @pl.when(t + 2 < nz)
        def _():
            second(t + 2)

        @pl.when(t + 1 < nz)
        def _():
            third(t + 1)

        rest(t)
        products(t)

        @pl.when(t == 0)
        def _():
            @pl.loop(0, 2)
            def _(way):
                send_on(t, way, way, nz // 2, False)

        @pl.when(jnp.logical_and(t > 0, t < nz - 1))
        def _():
            way = 1 - t % 2
            send_on(t, way, way, distance(t), True)

            @pl.when(t < 3)
            def _():
                send_on(t, way, 1 - way, distance(t), False)

            @pl.when(t >= 3)
            def _():
                send_on(t, way, 1 - way, distance(t), True)

    stores = []
    for h in range(2):
        arrived(0, h, 1)
        arrived(1, h, 1)
        for which in range(2):
            for j in range(cols // BLOCK):
                lanes = slice(which * cols + j * BLOCK, which * cols + (j + 1) * BLOCK)
                total = part[nz - 1, h, :, lanes] + decoded(slot_of(0, h, 1), lanes)
                total = total + decoded(slot_of(1, h, 1), lanes)
                keep_it = keep[h * half // BLOCK, j].astype(jnp.float32)
                stage[which, h, :, j * BLOCK : (j + 1) * BLOCK] = (total * keep_it).astype(jnp.bfloat16)
            out = (out_square, out_tangent)[which]
            store = pltpu.make_async_copy(stage.at[which, h], out.at[pl.ds(h * half, half)], store_sem.at[which, h])
            store.start()
            stores.append(store)

    for q in range(nc):

        @pl.when(jnp.logical_or(z != col, col != q))
        def _():
            scatter(q).wait_send()

    @pl.loop(0, nz)
    def _(t):
        for k, (q, c) in enumerate(
            ((col, partner), (col, up), (col, down), (partner, up), (partner, down), (from_down, up), (from_up, down))
        ):
            hand_on(t, q, c, k).wait_send()

    for way in range(2):
        for h in range(2):
            for d in range(1, nz // 2 + (1 if way == h else 0)):
                values_copy(way, h, d).wait_send()
                scales_copy(way, h, d).wait_send()
    for store in stores:
        store.wait()


def per_device(nz, nc, group, x0_rows, x1_rows, x0_cols, x1_cols, m0_rows, m1_rows, m0_cols, m1_cols, keep):
    rows = x0_rows.shape[0]
    depth, cols = x0_cols.shape
    piece, half, slots = rows // nc, rows // 2, 2 * nz
    hbm = pl.BlockSpec(memory_space=pl.ANY)
    smem = pl.BlockSpec(memory_space=pltpu.SMEM)
    dma = pltpu.SemaphoreType.DMA
    out = jax.ShapeDtypeStruct((rows, cols), jnp.bfloat16)
    return pl.pallas_call(
        functools.partial(kernel, group, nz, nc),
        out_shape=(out, out),
        in_specs=[hbm] * 4 + [smem] * 5,
        out_specs=(hbm, hbm),
        scratch_shapes=[
            pltpu.VMEM((nc, 2, piece, depth), jnp.bfloat16),
            pltpu.VMEM((nz, nc, 2, piece, depth), jnp.bfloat16),
            pltpu.VMEM((2, depth, cols), jnp.bfloat16),
            pltpu.VMEM((nz, 2, half, 2 * cols), jnp.float32),
            pltpu.VMEM((slots, half, 2 * cols), jnp.int16),
            pltpu.VMEM((slots, half, 2 * cols), jnp.int16),
            pltpu.VMEM((slots, 1, 2 * cols), jnp.float32),
            pltpu.VMEM((slots, 1, 2 * cols), jnp.float32),
            pltpu.VMEM((2, 2, half, cols), jnp.bfloat16),
            dma((2, nc)),
            dma((2,)),
            dma((nc,)),
            dma((nz, nc)),
            dma((nz, 7)),
            dma((slots,)),
            dma((slots,)),
            dma((slots,)),
            dma((slots,)),
            dma((2, 2)),
        ],
        compiler_params=pltpu.CompilerParams(
            collective_id=0, has_side_effects=True, vmem_limit_bytes=56 * 1024 * 1024
        ),
        name="window_kernel",
    )(x0_rows, x1_rows, x0_cols, x1_cols, m0_rows, m1_rows, m0_cols, m1_cols, keep)


def solution(mesh):
    nc = mesh.shape["col"]
    nz = 8
    group = mesh.shape["row"] // nz
    return jax.shard_map(
        functools.partial(per_device, nz, nc, group),
        mesh=mesh,
        in_specs=(P("row", "col"),) * 9,
        out_specs=(P("row", "col"), P("row", "col")),
        check_vma=False,
    )
```

time: 879 us -> 191 us (0.22)
  the two profiles are of different devices: /device:TPU:6 before, /device:TPU:64 now
where the time goes in v1:
time: 191 us
  Pallas kernels  187 us (98%)
  local copies, waits for them, and re-layouts  3.53 us (2%)
    pallas_call x1, Pallas kernels, per_device(): pl.pallas_call(functools.partial(kernel, group, nz, nc), out_shape=(out,...  187 us

profile of v1, /device:TPU:64, one launch (start us, length us, event | category | flops | bytes accessed | tf_op | source)
XLA Modules:
  0.0 191.1 jit_solution(13467122615146027512)
XLA Ops:
  0.6 186.9 %window_kernel.1 = (bf16[256,768]{1,0:T(8,128)(2,1)}, bf16[256,768]{1,0:T(8,128)(2,1)}) custom-call(bf16[256,4096]{1,0:T(8,128)(2,1)} %x0_rows.1, bf16[256,4096]{1,0:T(8,128)(2,1)} %x1_rows.1, bf16[1024,768]{1,0:T(8,128)(2,1)} %x0_cols.1, bf16[1024,768]{1,0:T(8,128)(2,1)} %x1_cols.1, s32[2,32]{1,0:T(2,128)} %m0_rows.1, s32[2,32]{1,0:T(2,128)} %m1_rows.1, ...), custom_call_target="tpu_custom_call" | custom-call | tf_op jit(solution)/shard_map/window_kernel/pallas_call | solution.py:314
  187.6 1.8 copy.13
  189.3 1.8 copy.14

commit v2 on v1

--- a/solution.py
+++ b/solution.py
@@ -17,8 +17,8 @@
     group, nz, nc,
     x0_rows, x1_rows, x0_cols, x1_cols, m0_rows, m1_rows, m0_cols, m1_cols, keep,
     out_square, out_tangent,
-    own, left, right, part, q_out, q_in, s_out, s_in, stage,
-    load_sem, load_right_sem, v_send, left_recv, g_send, q_send, q_recv, s_send, s_recv, store_sem,
+    own, middle, left, right, part, q_out, q_in, s_out, s_in, stage,
+    load_sem, load_right_sem, v_send, v_recv, m_send, left_recv, g_send, q_send, q_recv, s_send, s_recv, store_sem,
 ):
     rows, depth = own.shape[0] * own.shape[2], own.shape[3]
     piece = own.shape[2]
@@ -32,7 +32,6 @@
     partner = y * 2 + 1 - xh
     up_y, down_y = (y + 1) % ny, (y + ny - 1) % ny
     up, down = up_y * 2 + xh, down_y * 2 + xh
-    on_diagonal = z == col
 
     def left_load(which, source, q):
         return pltpu.make_async_copy(
@@ -51,16 +50,10 @@
     right_load(1, x1_cols).start()
 
     barrier = pltpu.get_barrier_semaphore()
-    for p in range(nz):
-
-        @pl.when(jnp.logical_or(z != p, z != col))
-        def _():
-            pl.semaphore_signal(barrier, inc=1, device_id=(p * group + s, z), device_id_type=MESH)
-
-    for c in (partner, up, down):
-        pl.semaphore_signal(barrier, inc=1, device_id=(row, c), device_id_type=MESH)
-    for zn in ((z + 1) % nz, (z + nz - 1) % nz):
-        pl.semaphore_signal(barrier, inc=1, device_id=(zn * group + s, col), device_id_type=MESH)
+    for i in range(1, nc):
+        pl.semaphore_signal(barrier, inc=1, device_id=(row, (col + i) % nc), device_id_type=MESH)
+    for i in range(1, nz):
+        pl.semaphore_signal(barrier, inc=1, device_id=((z + i) % nz * group + s, col), device_id_type=MESH)
 
     for q in range(nc):
         left_load(0, x0_rows, q).wait()
@@ -71,27 +64,47 @@
                 lanes = slice(j * BLOCK, (j + 1) * BLOCK)
                 own[q, which, :, lanes] = (own[q, which, :, lanes].astype(jnp.float32) * keep_it).astype(jnp.bfloat16)
 
-    pl.semaphore_wait(barrier, nz + 5 - jnp.where(on_diagonal, 1, 0))
-
-    def scatter(q):
+    pl.semaphore_wait(barrier, nc + nz - 2)
+
+    def scatter(i):
+        q = (col + i) % nc
         return pltpu.make_async_remote_copy(
             src_ref=own.at[q],
-            dst_ref=left.at[z, q],
-            send_sem=v_send.at[q],
-            recv_sem=left_recv.at[z, q],
-            device_id=(col * group + s, q),
-            device_id_type=MESH,
-        )
-
-    for q in range(nc):
-
-        @pl.when(jnp.logical_or(z != col, col != q))
-        def _():
-            scatter(q).start()
-
-    @pl.when(on_diagonal)
+            dst_ref=middle.at[col],
+            send_sem=v_send.at[i],
+            recv_sem=v_recv.at[col],
+            device_id=(row, q),
+            device_id_type=MESH,
+        )
+
+    def arrived_piece(j):
+        return pltpu.make_async_remote_copy(
+            src_ref=middle.at[j],
+            dst_ref=middle.at[j],
+            send_sem=v_send.at[0],
+            recv_sem=v_recv.at[j],
+            device_id=(row, j),
+            device_id_type=MESH,
+        )
+
+    def to_plane(j):
+        return pltpu.make_async_remote_copy(
+            src_ref=middle.at[j],
+            dst_ref=left.at[z, col],
+            send_sem=m_send.at[j],
+            recv_sem=left_recv.at[z, col, 0],
+            device_id=(j * group + s, col),
+            device_id_type=MESH,
+        )
+
+    for i in range(1, nc):
+        scatter(i).start()
+    middle[col] = own[col]
+
+    @pl.when(z != col)
     def _():
-        left[z, col] = own[col]
+        to_plane(col).start()
+
 
     right_load(0, x0_cols).wait()
     right_load(1, x1_cols).wait()
@@ -105,56 +118,103 @@
                 lanes = slice(j * BLOCK, (j + 1) * BLOCK)
                 right[which, span, lanes] = (right[which, span, lanes].astype(jnp.float32) * keep_it).astype(jnp.bfloat16)
 
-    def distance(t):
-        return nz // 2 - (t + 1) // 2
-
-    def panel(t):
-        ahead = t % 2
-        return (z + ahead * distance(t) + (1 - ahead) * (nz - distance(t))) % nz
-
-    def hand_on(t, q, c, k):
-        p = panel(t)
-        return pltpu.make_async_remote_copy(
-            src_ref=left.at[p, q],
-            dst_ref=left.at[p, q],
-            send_sem=g_send.at[t, k],
-            recv_sem=left_recv.at[p, q],
+    def onward(i):
+        j = (z + i) % nz
+
+        @pl.when(j != col)
+        def _():
+            arrived_piece(j).wait_recv()
+            to_plane(j).start()
+
+    onward(4)
+
+    @pl.when(z != col)
+    def _():
+        arrived_piece(z).wait_recv()
+
+    left[z, col] = middle[z]
+
+    def distance(g):
+        return nz // 2 - g // 2
+
+    def panel(g):
+        if isinstance(g, int) and g == 0:
+            return z
+        ahead = 1 - g % 2
+        return (z + ahead * distance(g) + (1 - ahead) * (nz - distance(g))) % nz
+
+    def hand_on(g, q, c, k, which=None):
+        p = panel(g)
+        ref = left.at[p, q] if which is None else left.at[p, q, which]
+        return pltpu.make_async_remote_copy(
+            src_ref=ref,
+            dst_ref=ref,
+            send_sem=g_send.at[g, k],
+            recv_sem=left_recv.at[p, q, 0 if which is None else which],
             device_id=(row, c),
             device_id_type=MESH,
         )
 
-    def first(t):
-        @pl.when(jnp.logical_or(panel(t) != z, z != col))
-        def _():
-            hand_on(t, col, partner, 0).wait_recv()
-
-        hand_on(t, col, up, 1).start()
-        hand_on(t, col, down, 2).start()
-        hand_on(t, col, partner, 0).start()
-
-    def second(t):
-        hand_on(t, partner, partner, 0).wait_recv()
-        hand_on(t, partner, up, 3).start()
-        hand_on(t, partner, down, 4).start()
-
+    def wait_piece(g, q, which=None):
+        hand_on(g, q, up, 0, which).wait_recv()
+
+    far_y = (y + 2) % ny
+    far, far_partner = far_y * 2 + xh, far_y * 2 + 1 - xh
+    up_partner, down_partner = up_y * 2 + 1 - xh, down_y * 2 + 1 - xh
     from_down, from_up = down_y * 2, up_y * 2 + 1
 
-    def third(t):
-        hand_on(t, from_down, up, 5).wait_recv()
-        hand_on(t, from_down, up, 5).start()
-        hand_on(t, from_up, down, 6).wait_recv()
-        hand_on(t, from_up, down, 6).start()
-
-    far_y = (y + 2) % ny
-
-    def rest(t):
-        for q in (down_y * 2 + 1, up_y * 2, far_y * 2, far_y * 2 + 1):
-            hand_on(t, q, up, 5).wait_recv()
+    def first(g):
+        if not (isinstance(g, int) and g == 0):
+            wait_piece(g, col)
+        hand_on(g, col, up, 0).start()
+        hand_on(g, col, down, 1).start()
+        hand_on(g, col, partner, 2).start()
+
+    def second(g):
+        turn = g // 2 % 2
+        wait_piece(g, up)
+        wait_piece(g, down)
+        hand_on(g, down * turn + up * (1 - turn), up * turn + down * (1 - turn), 3, 1).start()
+        hand_on(g, up, partner, 4, 1).start()
+        hand_on(g, down, partner, 5, 1).start()
+        wait_piece(g, partner)
+        hand_on(g, partner, up, 6, 0).start()
+        hand_on(g, partner, down, 7, 0).start()
+
+    def third(g):
+        wait_piece(g, far, 1)
+        hand_on(g, far, partner, 8, 1).start()
+
+        @pl.when(xh == 0)
+        def _():
+            wait_piece(g, up_partner, 0)
+
+        @pl.when(xh == 1)
+        def _():
+            wait_piece(g, down_partner, 0)
+
+        hand_on(g, from_down, up, 9, 0).start()
+        hand_on(g, from_up, down, 10, 0).start()
+
+    def rest(g):
+        @pl.when(xh == 1)
+        def _():
+            wait_piece(g, up_partner, 0)
+
+        @pl.when(xh == 0)
+        def _():
+            wait_piece(g, down_partner, 0)
+
+        wait_piece(g, up_partner, 1)
+        wait_piece(g, down_partner, 1)
+        wait_piece(g, far, 0)
+        wait_piece(g, far_partner, 0)
+        wait_piece(g, far_partner, 1)
 
     width = 256 if cols % 256 == 0 else BLOCK
 
-    def products(t):
-        p = panel(t)
+    def products(g):
+        p = panel(g)
 
         @pl.loop(0, cols // width)
         def _(n):
@@ -167,8 +227,8 @@
             tangent = jnp.dot(l0, r1, preferred_element_type=jnp.float32)
             tangent = tangent + jnp.dot(l1, r0, preferred_element_type=jnp.float32)
             for h in range(2):
-                part[t, h, :, pl.ds(start, width)] = square[h * half : (h + 1) * half]
-                part[t, h, :, pl.ds(cols + start, width)] = tangent[h * half : (h + 1) * half]
+                part[g, h, :, pl.ds(start, width)] = square[h * half : (h + 1) * half]
+                part[g, h, :, pl.ds(cols + start, width)] = tangent[h * half : (h + 1) * half]
 
     def slot_of(way, h, d):
         return (way * 2 + h) * (nz // 2) + d - 1
@@ -204,7 +264,7 @@
     def decoded(slot, lanes):
         return q_in[slot, :, lanes].astype(jnp.int32).astype(jnp.float32) * s_in[slot, :, lanes]
 
-    def send_on(t, way, h, d, adding):
+    def send_on(g, way, h, d, adding):
         slot = slot_of(way, h, d)
         if adding:
             arrived(way, h, d + 1)
@@ -212,7 +272,7 @@
         @pl.loop(0, 2 * cols // BLOCK)
         def _(j):
             lanes = pl.ds(pl.multiple_of(j * BLOCK, BLOCK), BLOCK)
-            total = part[t, h, :, lanes]
+            total = part[g, h, :, lanes]
             if adding:
                 total = total + decoded(slot + 1, lanes)
             top = jnp.maximum(jnp.max(jnp.abs(total), axis=0, keepdims=True), FLOOR)
@@ -222,48 +282,52 @@
         values_copy(way, h, d).start()
         scales_copy(way, h, d).start()
 
-    first(0)
-    first(1)
-    first(2)
-    second(0)
-    second(1)
-    third(0)
-
-    @pl.loop(0, nz)
-    def _(t):
-        @pl.when(t + 3 < nz)
-        def _():
-            first(t + 3)
-
-        @pl.when(t + 2 < nz)
-        def _():
-            second(t + 2)
-
-        @pl.when(t + 1 < nz)
-        def _():
-            third(t + 1)
-
-        rest(t)
-        products(t)
-
-        @pl.when(t == 0)
+    def stages(g):
+        for lag, stage_of in zip((0, 1, 2), (third, second, first)):
+            if isinstance(g, int):
+                if g + lag >= 0:
+                    stage_of(g + lag)
+            else:
+                pl.when(g + lag < nz)(functools.partial(stage_of, g + lag))
+
+    stages(-2)
+    onward(5)
+    onward(3)
+    stages(-1)
+    onward(6)
+    onward(2)
+    stages(0)
+    onward(7)
+    onward(1)
+
+    @pl.loop(1, nz)
+    def _(g):
+        stages(g)
+        rest(g)
+        products(g)
+
+        @pl.when(g == 1)
         def _():
             @pl.loop(0, 2)
             def _(way):
-                send_on(t, way, way, nz // 2, False)
-
-        @pl.when(jnp.logical_and(t > 0, t < nz - 1))
-        def _():
-            way = 1 - t % 2
-            send_on(t, way, way, distance(t), True)
-
-            @pl.when(t < 3)
+                send_on(g, way, way, nz // 2, False)
+
+        @pl.when(g > 1)
+        def _():
+            way = g % 2
+
+            @pl.when(g < 4)
             def _():
-                send_on(t, way, 1 - way, distance(t), False)
-
-            @pl.when(t >= 3)
+                send_on(g, way, 1 - way, distance(g), False)
+
+            @pl.when(g >= 4)
             def _():
-                send_on(t, way, 1 - way, distance(t), True)
+                send_on(g, way, 1 - way, distance(g), True)
+
+            send_on(g, way, way, distance(g), True)
+
+    rest(0)
+    products(0)
 
     stores = []
     for h in range(2):
@@ -272,7 +336,7 @@
         for which in range(2):
             for j in range(cols // BLOCK):
                 lanes = slice(which * cols + j * BLOCK, which * cols + (j + 1) * BLOCK)
-                total = part[nz - 1, h, :, lanes] + decoded(slot_of(0, h, 1), lanes)
+                total = part[0, h, :, lanes] + decoded(slot_of(0, h, 1), lanes)
                 total = total + decoded(slot_of(1, h, 1), lanes)
                 keep_it = keep[h * half // BLOCK, j].astype(jnp.float32)
                 stage[which, h, :, j * BLOCK : (j + 1) * BLOCK] = (total * keep_it).astype(jnp.bfloat16)
@@ -281,18 +345,17 @@
             store.start()
             stores.append(store)
 
-    for q in range(nc):
-
-        @pl.when(jnp.logical_or(z != col, col != q))
-        def _():
-            scatter(q).wait_send()
-
-    @pl.loop(0, nz)
-    def _(t):
-        for k, (q, c) in enumerate(
-            ((col, partner), (col, up), (col, down), (partner, up), (partner, down), (from_down, up), (from_up, down))
-        ):
-            hand_on(t, q, c, k).wait_send()
+    for i in range(1, nc):
+        scatter(i).wait_send()
+    for i in range(1, nz):
+        to_plane((z + i) % nz).wait_send()
+
+    def sent(g):
+        for k in range(11):
+            hand_on(g, col, up, k, None if k < 3 else 0).wait_send()
+
+    sent(0)
+    pl.loop(1, nz)(sent)
 
     for way in range(2):
         for h in range(2):
@@ -318,6 +381,7 @@
         out_specs=(hbm, hbm),
         scratch_shapes=[
             pltpu.VMEM((nc, 2, piece, depth), jnp.bfloat16),
+            pltpu.VMEM((nc, 2, piece, depth), jnp.bfloat16),
             pltpu.VMEM((nz, nc, 2, piece, depth), jnp.bfloat16),
             pltpu.VMEM((2, depth, cols), jnp.bfloat16),
             pltpu.VMEM((nz, 2, half, 2 * cols), jnp.float32),
@@ -329,8 +393,10 @@
             dma((2, nc)),
             dma((2,)),
             dma((nc,)),
-            dma((nz, nc)),
-            dma((nz, 7)),
+            dma((nc,)),
+            dma((nz,)),
+            dma((nz, nc, 2)),
+            dma((nz, 11)),
             dma((slots,)),
             dma((slots,)),
             dma((slots,)),

time: 191 us -> 129 us (0.68)
  the two profiles are of different devices: /device:TPU:64 before, /device:TPU:6 now
where the time goes in v2:
time: 129 us
  Pallas kernels  125 us (97%)
  local copies, waits for them, and re-layouts  3.53 us (3%)
    pallas_call x1, Pallas kernels, per_device(): pl.pallas_call(functools.partial(kernel, group, nz, nc), out_shape=(out,...  125 us
    unnamed x2, local copies, waits for them, and re-layouts  3.53 us

profile of v2, /device:TPU:6, one launch (start us, length us, event | category | flops | bytes accessed | tf_op | source)
XLA Modules:
  0.0 129.3 jit_solution(7981258956318809444)
XLA Ops:
  0.6 125.1 %window_kernel.1 = (bf16[256,768]{1,0:T(8,128)(2,1)}, bf16[256,768]{1,0:T(8,128)(2,1)}) custom-call(bf16[256,4096]{1,0:T(8,128)(2,1)} %x0_rows.1, bf16[256,4096]{1,0:T(8,128)(2,1)} %x1_rows.1, bf16[1024,768]{1,0:T(8,128)(2,1)} %x0_cols.1, bf16[1024,768]{1,0:T(8,128)(2,1)} %x1_cols.1, s32[2,32]{1,0:T(2,128)} %m0_rows.1, s32[2,32]{1,0:T(2,128)} %m1_rows.1, ...), custom_call_target="tpu_custom_call" | custom-call | tf_op jit(solution)/shard_map/window_kernel/pallas_call | solution.py:377
  125.7 1.8 %copy.13 = bf16[256,768]{1,0:T(8,128)(2,1)} copy(bf16[256,768]{1,0:T(8,128)(2,1)} %get-tuple-element.4) | data formatting | bytes 786432
  127.5 1.8 %copy.14 = bf16[256,768]{1,0:T(8,128)(2,1)} copy(bf16[256,768]{1,0:T(8,128)(2,1)} %get-tuple-element.5) | data formatting | bytes 786432

commit v3 on v2

v3 whole, which is shorter than its diff:
```python
import functools

import jax
import jax.numpy as jnp
from jax import lax
from jax.experimental import pallas as pl
from jax.experimental.pallas import tpu as pltpu
from jax.sharding import PartitionSpec as P

BLOCK = 128
LEVELS = 32760.0
FLOOR = 1e-33
MESH = pl.DeviceIdType.MESH


def kernel(
    group, nz, nc,
    x0_rows, x1_rows, x0_cols, x1_cols, m0_rows, m1_rows, m0_cols, m1_cols, keep,
    out_square, out_tangent,
    own, middle, left, right, part, q_out, q_in, s_out, s_in, stage,
    load_sem, load_right_sem, v_send, v_recv, m_send, left_recv, g_send, q_send, q_recv, s_send, s_recv, store_sem,
):
    thin, depth = own.shape[3], own.shape[4]
    rows = nc * 2 * thin
    half = rows // 2
    cols = right.shape[2]
    row = lax.axis_index("row")
    col = lax.axis_index("col")
    z, s = row // group, row % group
    y, xh = col // 2, col % 2
    ny = nc // 2
    partner = y * 2 + 1 - xh
    up_y, down_y = (y + 1) % ny, (y + ny - 1) % ny
    up, down = up_y * 2 + xh, down_y * 2 + xh
    ahead = (col + nz - z) % nz

    barrier = pltpu.get_barrier_semaphore()
    for i in range(1, nc):
        pl.semaphore_signal(barrier, inc=1, device_id=(row, (col + i) % nc), device_id_type=MESH)
    for i in range(1, nz):
        pl.semaphore_signal(barrier, inc=1, device_id=((z + i) % nz * group + s, col), device_id_type=MESH)

    def left_load(which, source):
        return pltpu.make_async_copy(
            source.at[:, :, :, pl.ds(pl.multiple_of(s * depth, depth), depth)],
            own.at[:, :, which],
            load_sem.at[which],
        )

    def right_load(which, source):
        return pltpu.make_async_copy(source, right.at[which], load_right_sem.at[which])

    left_load(0, x0_rows).start()
    left_load(1, x1_rows).start()
    right_load(0, x0_cols).start()
    right_load(1, x1_cols).start()

    for which, (source, mask) in enumerate(((x0_rows, m0_rows), (x1_rows, m1_rows))):
        left_load(which, source).wait()
        for q in range(nc):
            for j in range(depth // BLOCK):
                keep_it = mask[q * 2 * thin // BLOCK, s * (depth // BLOCK) + j].astype(jnp.float32)
                lanes = slice(j * BLOCK, (j + 1) * BLOCK)
                own[q, :, which, :, lanes] = (own[q, :, which, :, lanes].astype(jnp.float32) * keep_it).astype(jnp.bfloat16)

    pl.semaphore_wait(barrier, nc + nz - 2)

    def copy_of(q, target, recv, k, device_row):
        return pltpu.make_async_remote_copy(
            src_ref=own.at[q],
            dst_ref=target,
            send_sem=v_send.at[k],
            recv_sem=recv,
            device_id=(device_row, q),
            device_id_type=MESH,
        )

    def scatter(k):
        q = (col + k) % nc
        return copy_of(q, middle.at[col], v_recv.at[col], k, row)

    def scatter_own(k):
        q = (col + k) % nc
        return copy_of(q, left.at[0, :, q], left_recv.at[0, q, 0], k, row)

    @pl.when(ahead == 0)
    def _():
        for k in range(1, nc):
            scatter_own(k).start()
        left[0, :, col] = own[col]

    @pl.when(ahead != 0)
    def _():
        for k in range(1, nc):
            scatter(k).start()
        middle[col] = own[col]

    def arrived_piece(j):
        return pltpu.make_async_remote_copy(
            src_ref=middle.at[j],
            dst_ref=middle.at[j],
            send_sem=v_send.at[0],
            recv_sem=v_recv.at[j],
            device_id=(row, j),
            device_id_type=MESH,
        )

    def to_plane(i, h):
        d = min(i, nz - i)
        if i == nz // 2:
            return pltpu.make_async_remote_copy(
                src_ref=middle.at[(z + i) % nz],
                dst_ref=left.at[1, :, col],
                send_sem=m_send.at[i, 0],
                recv_sem=left_recv.at[1, col, 0],
                device_id=((z + i) % nz * group + s, col),
                device_id_type=MESH,
            )
        u, b = 2 * (nz // 2 - d) + h, 1 if i < nz // 2 else 0
        j = (z + i) % nz
        return pltpu.make_async_remote_copy(
            src_ref=middle.at[j, h],
            dst_ref=left.at[u, b, col],
            send_sem=m_send.at[i, h],
            recv_sem=left_recv.at[u, col, b],
            device_id=(j * group + s, col),
            device_id_type=MESH,
        )

    for i in range(1, nz):

        @pl.when(ahead == i)
        def _():
            for h in range(1 if i == nz // 2 else 2):
                to_plane(i, h).start()

    right_load(0, x0_cols).wait()
    right_load(1, x1_cols).wait()

    @pl.loop(0, depth // BLOCK)
    def _(i):
        span = pl.ds(pl.multiple_of(i * BLOCK, BLOCK), BLOCK)
        for which, mask in enumerate((m0_cols, m1_cols)):
            for j in range(cols // BLOCK):
                keep_it = mask[i, j].astype(jnp.float32)
                lanes = slice(j * BLOCK, (j + 1) * BLOCK)
                right[which, span, lanes] = (right[which, span, lanes].astype(jnp.float32) * keep_it).astype(jnp.bfloat16)

    def onward(i, h):
        @pl.when(ahead != i)
        def _():
            if h == 0:
                arrived_piece((z + i) % nz).wait_recv()
            to_plane(i, h).start()

    def hand_on(u, q, c, k, which=None):
        ref = left.at[u, :, q] if which is None else left.at[u, :, q, which]
        return pltpu.make_async_remote_copy(
            src_ref=ref,
            dst_ref=ref,
            send_sem=g_send.at[u, k],
            recv_sem=left_recv.at[u, q, 0 if which is None else which],
            device_id=(row, c),
            device_id_type=MESH,
        )

    def wait_piece(u, q, which=None):
        hand_on(u, q, up, 0, which).wait_recv()

    def wait_half(u, b):
        pltpu.make_async_remote_copy(
            src_ref=left.at[u, b, col],
            dst_ref=left.at[u, b, col],
            send_sem=m_send.at[1, 0],
            recv_sem=left_recv.at[u, col, b],
            device_id=(row, up),
            device_id_type=MESH,
        ).wait_recv()

    far_y = (y + 2) % ny
    far, far_partner = far_y * 2 + xh, far_y * 2 + 1 - xh
    up_partner, down_partner = up_y * 2 + 1 - xh, down_y * 2 + 1 - xh
    from_down, from_up = down_y * 2, up_y * 2 + 1

    def first(u):
        if isinstance(u, int) and u == 0:

            @pl.when(ahead != 0)
            def _():
                wait_piece(u, col)

        elif isinstance(u, int) and u == 1:
            wait_piece(u, col)
        else:
            wait_half(u, 0)
            wait_half(u, 1)
        hand_on(u, col, up, 0).start()
        hand_on(u, col, down, 1).start()
        hand_on(u, col, partner, 2).start()

    def second(u):
        turn = u // 2 % 2
        wait_piece(u, up)
        wait_piece(u, down)
        hand_on(u, down * turn + up * (1 - turn), up * turn + down * (1 - turn), 3, 1).start()
        hand_on(u, up, partner, 4, 1).start()
        hand_on(u, down, partner, 5, 1).start()
        wait_piece(u, partner)
        hand_on(u, partner, up, 6, 0).start()
        hand_on(u, partner, down, 7, 0).start()

    def third(u):
        wait_piece(u, far, 1)
        hand_on(u, far, partner, 8, 1).start()

        @pl.when(xh == 0)
        def _():
            wait_piece(u, up_partner, 0)

        @pl.when(xh == 1)
        def _():
            wait_piece(u, down_partner, 0)

        hand_on(u, from_down, up, 9, 0).start()
        hand_on(u, from_up, down, 10, 0).start()

    def rest(u):
        @pl.when(xh == 1)
        def _():
            wait_piece(u, up_partner, 0)

        @pl.when(xh == 0)
        def _():
            wait_piece(u, down_partner, 0)

        wait_piece(u, up_partner, 1)
        wait_piece(u, down_partner, 1)
        wait_piece(u, far, 0)
        wait_piece(u, far_partner, 0)
        wait_piece(u, far_partner, 1)

    width = 256 if cols % 256 == 0 else BLOCK

    def products(u):

        @pl.loop(0, cols // width)
        def _(n):
            start = pl.multiple_of(n * width, width)
            l0 = left[u, :, :, 0].reshape(rows, depth)
            l1 = left[u, :, :, 1].reshape(rows, depth)
            r0 = right[0, :, pl.ds(start, width)]
            r1 = right[1, :, pl.ds(start, width)]
            square = jnp.dot(l0, r0, preferred_element_type=jnp.float32)
            tangent = jnp.dot(l0, r1, preferred_element_type=jnp.float32)
            tangent = tangent + jnp.dot(l1, r0, preferred_element_type=jnp.float32)
            for b in range(2):
                part[u, b, :, pl.ds(start, width)] = square[b * half : (b + 1) * half]
                part[u, b, :, pl.ds(cols + start, width)] = tangent[b * half : (b + 1) * half]

    def slot_of(way, h, d):
        return (way * 2 + h) * (nz // 2) + d - 1

    def values_copy(way, h, d):
        slot = slot_of(way, h, d)
        zn = (z + 1 + way * (nz - 2)) % nz
        return pltpu.make_async_remote_copy(
            src_ref=q_out.at[slot],
            dst_ref=q_in.at[slot],
            send_sem=q_send.at[slot],
            recv_sem=q_recv.at[slot],
            device_id=(zn * group + s, col),
            device_id_type=MESH,
        )

    def scales_copy(way, h, d):
        slot = slot_of(way, h, d)
        zn = (z + 1 + way * (nz - 2)) % nz
        return pltpu.make_async_remote_copy(
            src_ref=s_out.at[slot],
            dst_ref=s_in.at[slot],
            send_sem=s_send.at[slot],
            recv_sem=s_recv.at[slot],
            device_id=(zn * group + s, col),
            device_id_type=MESH,
        )

    def arrived(way, h, d):
        values_copy(way, h, d).wait_recv()
        scales_copy(way, h, d).wait_recv()

    def decoded(slot, lanes):
        return q_in[slot, :, lanes].astype(jnp.int32).astype(jnp.float32) * s_in[slot, :, lanes]

    def send_on(u, b, way, h, d, adding):
        slot = slot_of(way, h, d)
        if adding:
            arrived(way, h, d + 1)

        @pl.loop(0, 2 * cols // BLOCK)
        def _(j):
            lanes = pl.ds(pl.multiple_of(j * BLOCK, BLOCK), BLOCK)
            total = part[u, b, :, lanes]
            if adding:
                total = total + decoded(slot + 1, lanes)
            top = jnp.maximum(jnp.max(jnp.abs(total), axis=0, keepdims=True), FLOOR)
            q_out[slot, :, lanes] = jnp.round(total * (LEVELS / top)).astype(jnp.int32).astype(jnp.int16)
            s_out[slot, :, lanes] = top * (1.0 / LEVELS)

        values_copy(way, h, d).start()
        scales_copy(way, h, d).start()

    def ring_step(u):
        h, d = u % 2, nz // 2 - u // 2

        @pl.when(u < 4)
        def _():
            send_on(u, 1 - h, 1 - h, h, d, False)

        @pl.when(u >= 4)
        def _():
            send_on(u, 1 - h, 1 - h, h, d, True)

        send_on(u, h, h, h, d, True)

    def if_any(stage, u):
        pl.when(u < nz)(functools.partial(stage, u))

    onward(4, 0)
    first(0)
    onward(5, 0)
    onward(3, 0)
    second(0)
    first(1)
    onward(5, 1)
    onward(3, 1)
    onward(6, 0)
    onward(2, 0)
    third(0)
    second(1)
    first(2)
    onward(6, 1)
    onward(2, 1)
    onward(7, 0)
    onward(1, 0)
    onward(7, 1)
    onward(1, 1)
    third(1)
    second(2)
    first(3)
    rest(1)
    products(1)
    send_on(1, 0, 0, 0, nz // 2, False)
    send_on(1, 1, 1, 1, nz // 2, False)

    @pl.loop(2, nz)
    def _(u):
        third(u)
        if_any(second, u + 1)
        if_any(first, u + 2)
        rest(u)
        products(u)
        ring_step(u)

    rest(0)
    products(0)

    for h in range(2):
        arrived(0, h, 1)
        arrived(1, h, 1)
        for which in range(2):
            for j in range(cols // BLOCK):
                lanes = slice(which * cols + j * BLOCK, which * cols + (j + 1) * BLOCK)
                total = part[0, h, :, lanes] + decoded(slot_of(0, h, 1), lanes)
                total = total + decoded(slot_of(1, h, 1), lanes)
                total = total.reshape(nc, thin, BLOCK)
                per_block = BLOCK // (2 * thin)
                for i in range(nc // per_block):
                    keep_it = keep[i, j].astype(jnp.float32)
                    span = slice(i * per_block, (i + 1) * per_block)
                    stage[which, span, h, :, j * BLOCK : (j + 1) * BLOCK] = (total[span] * keep_it).astype(jnp.bfloat16)

    stores = []
    for which, out in enumerate((out_square, out_tangent)):
        store = pltpu.make_async_copy(stage.at[which], out, store_sem.at[which])
        store.start()
        stores.append(store)

    for k in range(1, nc):
        scatter(k).wait_send()
    for i in range(1, nz):
        for h in range(1 if i == nz // 2 else 2):
            to_plane(i, h).wait_send()

    def sent(u):
        for k in range(11):
            hand_on(u, col, up, k, None if k < 3 else 0).wait_send()

    pl.loop(0, nz)(sent)

    for way in range(2):
        for h in range(2):
            for d in range(1, nz // 2 + (1 if way == h else 0)):
                values_copy(way, h, d).wait_send()
                scales_copy(way, h, d).wait_send()
    for store in stores:
        store.wait()


def per_device(nz, nc, group, x0_rows, x1_rows, x0_cols, x1_cols, m0_rows, m1_rows, m0_cols, m1_cols, keep):
    rows = x0_rows.shape[0]
    depth, cols = x0_cols.shape
    thin, half, slots = rows // (2 * nc), rows // 2, 2 * nz
    x0_rows, x1_rows = (x.reshape(nc, 2, thin, -1) for x in (x0_rows, x1_rows))
    hbm = pl.BlockSpec(memory_space=pl.ANY)
    smem = pl.BlockSpec(memory_space=pltpu.SMEM)
    dma = pltpu.SemaphoreType.DMA
    out = jax.ShapeDtypeStruct((nc, 2, thin, cols), jnp.bfloat16)
    square, tangent = pl.pallas_call(
        functools.partial(kernel, group, nz, nc),
        out_shape=(out, out),
        in_specs=[hbm] * 4 + [smem] * 5,
        out_specs=(hbm, hbm),
        scratch_shapes=[
            pltpu.VMEM((nc, 2, 2, thin, depth), jnp.bfloat16),
            pltpu.VMEM((nc, 2, 2, thin, depth), jnp.bfloat16),
            pltpu.VMEM((nz, 2, nc, 2, thin, depth), jnp.bfloat16),
            pltpu.VMEM((2, depth, cols), jnp.bfloat16),
            pltpu.VMEM((nz, 2, half, 2 * cols), jnp.float32),
            pltpu.VMEM((slots, half, 2 * cols), jnp.int16),
            pltpu.VMEM((slots, half, 2 * cols), jnp.int16),
            pltpu.VMEM((slots, 1, 2 * cols), jnp.float32),
            pltpu.VMEM((slots, 1, 2 * cols), jnp.float32),
            pltpu.VMEM((2, nc, 2, thin, cols), jnp.bfloat16),
            dma((2,)),
            dma((2,)),
            dma((nc,)),
            dma((nc,)),
            dma((nz, 2)),
            dma((nz, nc, 2)),
            dma((nz, 11)),
            dma((slots,)),
            dma((slots,)),
            dma((slots,)),
            dma((slots,)),
            dma((2,)),
        ],
        compiler_params=pltpu.CompilerParams(
            collective_id=0, has_side_effects=True, vmem_limit_bytes=56 * 1024 * 1024
        ),
        name="window_kernel",
    )(x0_rows, x1_rows, x0_cols, x1_cols, m0_rows, m1_rows, m0_cols, m1_cols, keep)
    return square.reshape(rows, cols), tangent.reshape(rows, cols)


def solution(mesh):
    nc = mesh.shape["col"]
    nz = 8
    group = mesh.shape["row"] // nz
    return jax.shard_map(
        functools.partial(per_device, nz, nc, group),
        mesh=mesh,
        in_specs=(P("row", "col"),) * 9,
        out_specs=(P("row", "col"), P("row", "col")),
        check_vma=False,
    )
```

time: 129 us -> 122 us (0.946); the launches traced: 129 us -> 120 us
  Pallas kernels: 125 us -> 116 us
    pallas_call x1, Pallas kernels: 125 us -> 116 us  [per_device(): pl.pallas_call(functools.partial(kernel, group, nz, nc), out_shape=(out,...]
where the time goes in v3:
time: 122 us; the launch traced here: 120 us
  Pallas kernels  116 us (95%)
  local copies, waits for them, and re-layouts  3.53 us (3%)
    pallas_call x1, Pallas kernels, per_device(): pl.pallas_call(functools.partial(kernel, group, nz, nc), out_shape=(out,...  116 us
    unnamed x2, local copies, waits for them, and re-layouts  3.53 us

profile of v3, /device:TPU:6, one launch (start us, length us, event | category | flops | bytes accessed | tf_op | source)
XLA Modules:
  0.0 120.4 jit_solution(18306310812504832349)
XLA Ops:
  0.6 116.3 %window_kernel.1 = (bf16[8,2,16,768]{3,2,1,0:T(8,128)(2,1)}, bf16[8,2,16,768]{3,2,1,0:T(8,128)(2,1)}) custom-call(bf16[8,2,16,4096]{3,2,1,0:T(8,128)(2,1)} %bitcast.4, bf16[8,2,16,4096]{3,2,1,0:T(8,128)(2,1)} %bitcast.5, bf16[1024,768]{1,0:T(8,128)(2,1)} %x0_cols.1, bf16[1024,768]{1,0:T(8,128)(2,1)} %x1_cols.1, s32[2,32]{1,0:T(2,128)} %m0_rows.1, ...), custom_call_target="tpu_custom_call" | custom-call | tf_op jit(solution)/shard_map/window_kernel/pallas_call | solution.py:418
  116.9 1.8 %copy.13 = bf16[256,768]{1,0:T(8,128)(2,1)} copy(bf16[256,768]{1,0:T(8,128)(2,1)} %bitcast.7) | data formatting | bytes 786432
  118.7 1.8 %copy.14 = bf16[256,768]{1,0:T(8,128)(2,1)} copy(bf16[256,768]{1,0:T(8,128)(2,1)} %bitcast.6) | data formatting | bytes 786432

commit v4 on v3

--- a/solution.py
+++ b/solution.py
@@ -35,10 +35,10 @@
     ahead = (col + nz - z) % nz
 
     barrier = pltpu.get_barrier_semaphore()
+    for i in range(1, nz):
+        pl.semaphore_signal(barrier, inc=1, device_id=((z + i) % nz * group + s, col), device_id_type=MESH)
     for i in range(1, nc):
         pl.semaphore_signal(barrier, inc=1, device_id=(row, (col + i) % nc), device_id_type=MESH)
-    for i in range(1, nz):
-        pl.semaphore_signal(barrier, inc=1, device_id=((z + i) % nz * group + s, col), device_id_type=MESH)
 
     def left_load(which, source):
         return pltpu.make_async_copy(
@@ -327,30 +327,30 @@
 
     onward(4, 0)
     first(0)
+    second(0)
+    first(1)
     onward(5, 0)
     onward(3, 0)
-    second(0)
-    first(1)
+    second(1)
     onward(5, 1)
     onward(3, 1)
+    third(1)
     onward(6, 0)
     onward(2, 0)
-    third(0)
-    second(1)
-    first(2)
     onward(6, 1)
     onward(2, 1)
+    first(2)
+    rest(1)
+    products(1)
+    send_on(1, 0, 0, 0, nz // 2, False)
+    send_on(1, 1, 1, 1, nz // 2, False)
+    second(2)
+    first(3)
+    third(0)
     onward(7, 0)
     onward(1, 0)
     onward(7, 1)
     onward(1, 1)
-    third(1)
-    second(2)
-    first(3)
-    rest(1)
-    products(1)
-    send_on(1, 0, 0, 0, nz // 2, False)
-    send_on(1, 1, 1, 1, nz // 2, False)
 
     @pl.loop(2, nz)
     def _(u):
@@ -404,6 +404,11 @@
                 scales_copy(way, h, d).wait_send()
     for store in stores:
         store.wait()
+
+
+def hand_out(square, tangent, out_square, out_tangent):
+    out_square[...] = square[...]
+    out_tangent[...] = tangent[...]
 
 
 def per_device(nz, nc, group, x0_rows, x1_rows, x0_cols, x1_cols, m0_rows, m1_rows, m0_cols, m1_cols, keep):
@@ -449,7 +454,11 @@
         ),
         name="window_kernel",
     )(x0_rows, x1_rows, x0_cols, x1_cols, m0_rows, m1_rows, m0_cols, m1_cols, keep)
-    return square.reshape(rows, cols), tangent.reshape(rows, cols)
+    return pl.pallas_call(
+        hand_out,
+        out_shape=(jax.ShapeDtypeStruct((rows, cols), jnp.bfloat16),) * 2,
+        name="hand_out",
+    )(square.reshape(rows, cols), tangent.reshape(rows, cols))
 
 
 def solution(mesh):

time: 122 us -> 118 us (0.967)
  local copies, waits for them, and re-layouts: 3.53 us -> 0 us
    unnamed x2 -> x0, local copies, waits for them, and re-layouts: 3.53 us -> none
    pallas_call x1, Pallas kernels: 116 us -> 114 us  [per_device(): pl.pallas_call(functools.partial(kernel, group, nz, nc), out_shape=(out,...]
    pallas_call x0 -> x1, Pallas kernels: none -> 2.02 us  [per_device(): pl.pallas_call(hand_out, out_shape=(jax.ShapeDtypeStruct((rows, cols), jn...]
where the time goes in v4:
time: 118 us; the launch traced here: 116 us
  Pallas kernels  116 us (98%)
    pallas_call x1, Pallas kernels, per_device(): pl.pallas_call(functools.partial(kernel, group, nz, nc), out_shape=(out,...  114 us

profile of v4, /device:TPU:6, one launch (start us, length us, event | category | flops | bytes accessed | tf_op | source)
XLA Modules:
  0.0 116.5 jit_solution(6285686956400143502)
XLA Ops:
  0.6 113.8 %window_kernel.1 = (bf16[8,2,16,768]{3,2,1,0:T(8,128)(2,1)}, bf16[8,2,16,768]{3,2,1,0:T(8,128)(2,1)}) custom-call(bf16[8,2,16,4096]{3,2,1,0:T(8,128)(2,1)} %bitcast.4, bf16[8,2,16,4096]{3,2,1,0:T(8,128)(2,1)} %bitcast.5, bf16[1024,768]{1,0:T(8,128)(2,1)} %x0_cols.1, bf16[1024,768]{1,0:T(8,128)(2,1)} %x1_cols.1, s32[2,32]{1,0:T(2,128)} %m0_rows.1, ...), custom_call_target="tpu_custom_call" | custom-call | tf_op jit(solution)/shard_map/window_kernel/pallas_call | solution.py:423
  114.5 2.0 %hand_out.1 = (bf16[256,768]{1,0:T(8,128)(2,1)}, bf16[256,768]{1,0:T(8,128)(2,1)}) custom-call(bf16[256,768]{1,0:T(8,128)(2,1)} %bitcast.6, bf16[256,768]{1,0:T(8,128)(2,1)} %bitcast.7), custom_call_target="tpu_custom_call" | custom-call | tf_op jit(solution)/shard_map/hand_out/pallas_call | solution.py:457

commit v5 on v4

--- a/solution.py
+++ b/solution.py
@@ -83,18 +83,6 @@
         q = (col + k) % nc
         return copy_of(q, left.at[0, :, q], left_recv.at[0, q, 0], k, row)
 
-    @pl.when(ahead == 0)
-    def _():
-        for k in range(1, nc):
-            scatter_own(k).start()
-        left[0, :, col] = own[col]
-
-    @pl.when(ahead != 0)
-    def _():
-        for k in range(1, nc):
-            scatter(k).start()
-        middle[col] = own[col]
-
     def arrived_piece(j):
         return pltpu.make_async_remote_copy(
             src_ref=middle.at[j],
@@ -127,24 +115,47 @@
             device_id_type=MESH,
         )
 
-    for i in range(1, nz):
-
-        @pl.when(ahead == i)
-        def _():
-            for h in range(1 if i == nz // 2 else 2):
-                to_plane(i, h).start()
-
-    right_load(0, x0_cols).wait()
-    right_load(1, x1_cols).wait()
-
-    @pl.loop(0, depth // BLOCK)
-    def _(i):
+    def mask_right(i):
         span = pl.ds(pl.multiple_of(i * BLOCK, BLOCK), BLOCK)
         for which, mask in enumerate((m0_cols, m1_cols)):
             for j in range(cols // BLOCK):
                 keep_it = mask[i, j].astype(jnp.float32)
                 lanes = slice(j * BLOCK, (j + 1) * BLOCK)
                 right[which, span, lanes] = (right[which, span, lanes].astype(jnp.float32) * keep_it).astype(jnp.bfloat16)
+
+    def scatter_all():
+        for k in range(1, nc):
+            scatter(k).start()
+        middle[col] = own[col]
+
+    @pl.when(ahead == nz // 2)
+    def _():
+        scatter_all()
+        to_plane(nz // 2, 0).start()
+
+    right_load(0, x0_cols).wait()
+    right_load(1, x1_cols).wait()
+    pl.loop(0, 4)(mask_right)
+
+    @pl.when(ahead == 0)
+    def _():
+        for k in range(1, nc):
+            scatter_own(k).start()
+        left[0, :, col] = own[col]
+
+    @pl.when(ahead % (nz // 2) != 0)
+    def _():
+        scatter_all()
+
+    for i in range(1, nz):
+        if i != nz // 2:
+
+            @pl.when(ahead == i)
+            def _():
+                for h in range(2):
+                    to_plane(i, h).start()
+
+    pl.loop(4, depth // BLOCK)(mask_right)
 
     def onward(i, h):
         @pl.when(ahead != i)
@@ -344,13 +355,13 @@
     products(1)
     send_on(1, 0, 0, 0, nz // 2, False)
     send_on(1, 1, 1, 1, nz // 2, False)
-    second(2)
-    first(3)
-    third(0)
     onward(7, 0)
     onward(1, 0)
     onward(7, 1)
     onward(1, 1)
+    second(2)
+    first(3)
+    third(0)
 
     @pl.loop(2, nz)
     def _(u):

time: 118 us -> 118 us (level); the launches traced: 116 us -> 118 us
    pallas_call x1, Pallas kernels: 114 us -> 115 us  [per_device(): pl.pallas_call(functools.partial(kernel, group, nz, nc), out_shape=(out,...]
where the time goes in v5:
time: 118 us
  Pallas kernels  117 us (99%)
    pallas_call x1, Pallas kernels, per_device(): pl.pallas_call(functools.partial(kernel, group, nz, nc), out_shape=(out,...  115 us

profile of v5, /device:TPU:6, one launch (start us, length us, event | category | flops | bytes accessed | tf_op | source)
XLA Modules:
  0.0 117.7 jit_solution(3369679500777490884)
XLA Ops:
  0.6 115.0 %window_kernel.1 = (bf16[8,2,16,768]{3,2,1,0:T(8,128)(2,1)}, bf16[8,2,16,768]{3,2,1,0:T(8,128)(2,1)}) custom-call(bf16[8,2,16,4096]{3,2,1,0:T(8,128)(2,1)} %bitcast.4, bf16[8,2,16,4096]{3,2,1,0:T(8,128)(2,1)} %bitcast.5, bf16[1024,768]{1,0:T(8,128)(2,1)} %x0_cols.1, bf16[1024,768]{1,0:T(8,128)(2,1)} %x1_cols.1, s32[2,32]{1,0:T(2,128)} %m0_rows.1, ...), custom_call_target="tpu_custom_call" | custom-call | tf_op jit(solution)/shard_map/window_kernel/pallas_call | solution.py:434
  115.7 2.0 %hand_out.1 = (bf16[256,768]{1,0:T(8,128)(2,1)}, bf16[256,768]{1,0:T(8,128)(2,1)}) custom-call(bf16[256,768]{1,0:T(8,128)(2,1)} %bitcast.6, bf16[256,768]{1,0:T(8,128)(2,1)} %bitcast.7), custom_call_target="tpu_custom_call" | custom-call | tf_op jit(solution)/shard_map/hand_out/pallas_call | solution.py:468
